TPU v7x, 128 devices: a whole 4x4x4 slice. The times are simulated.
128 devices in a mesh: row: 16 (over x, z), col: 8 (over y, core).
Axes of the slice: x: 4, y: 4, z: 4, core: 2. Of those that a mesh axis runs over, the one named last changes fastest.
Arguments:
- primal_rows: bfloat16 [16384, 8192], P('row', 'col'), may hold values from -6 to 6
- dual_rows: bfloat16 [16384, 8192], P('row', 'col'), may hold values from -6 to 6
- weight_rows: bfloat16 [16384, 8192], P('row', 'col'), may hold values from -0.0625 to 0.0625
- pairs: int32 [384, 2], P('row'), may hold values from 0 to 63, as said below
Outputs:
- tiles: float32 [384, 256, 256], P('row', 'col')
Inputs may be any that keep to these rules, and one draw needn't show every extreme that they name: `pairs`: tile rows r * 24 to (r + 1) * 24 - 1 have their first block i among blocks r * 4 to (r + 1) * 4 - 1. Among their second blocks j, the blocks held by any other row index q (blocks q * 4 to (q + 1) * 4 - 1) are exactly one block, named one or more times; blocks of r itself may appear too.
All inputs are finite; a program needn't handle non-finite values.
Results may differ from a plain program's by a relative error of at most 0.0003.
Values may be sent and summed in bfloat16 or wider, within the bound.
No kernel may reach another device: no remote copies, remote signals or barrier semaphores. Data moves between devices by JAX's collectives and lax.ppermute only.
A program may use at most 128 MiB of HBM per device.

v0:
```python
import jax
import jax.numpy as jnp
from jax import lax
from jax.sharding import PartitionSpec as P

TILE = 256


def shards(primal_rows, dual_rows, weight_rows, pairs):
    row_count = lax.axis_size("row")
    my_row = lax.axis_index("row")
    per_row = primal_rows.shape[0] // TILE
    features = primal_rows.shape[1]
    tile_count = pairs.shape[0]
    every_pair = lax.all_gather(pairs, "row", axis=0, tiled=True)
    wanted = every_pair.reshape(row_count, tile_count * 2)
    held_here = wanted // per_row == my_row
    local_pick = jnp.max(jnp.where(held_here, wanted - my_row * per_row, 0), axis=1)
    weight_blocks = weight_rows.reshape(per_row, TILE, features)
    outgoing = jnp.take(weight_blocks, local_pick, axis=0)
    incoming = lax.all_to_all(outgoing, "row", split_axis=0, concat_axis=0, tiled=True)
    block_table = jnp.concatenate([weight_blocks, incoming], axis=0)
    first_local = pairs[:, 0] - my_row * per_row
    second_block = pairs[:, 1]
    second_row = second_block // per_row
    second_slot = jnp.where(
        second_row == my_row, second_block - my_row * per_row, per_row + second_row
    )
    left_x = jnp.take(primal_rows.reshape(per_row, TILE, features), first_local, axis=0)
    left_s = jnp.take(dual_rows.reshape(per_row, TILE, features), first_local, axis=0)
    right_rows = jnp.take(block_table, second_slot, axis=0)
    cross_x = jnp.einsum("tak,tbk->tab", left_x, right_rows, preferred_element_type=jnp.float32)
    cross_s = jnp.einsum("tak,tbk->tab", left_s, right_rows, preferred_element_type=jnp.float32)
    stacked = jnp.stack([cross_x, cross_s])
    whole = lax.psum(stacked, "col")
    slice_rows = TILE // lax.axis_size("col")
    summed = lax.dynamic_slice_in_dim(whole, lax.axis_index("col") * slice_rows, slice_rows, 2)
    return summed[0] * summed[1]


def solution(mesh):
    placed = (P("row", "col"), P("row", "col"), P("row", "col"), P("row", None))
    return jax.shard_map(
        shards, mesh=mesh, in_specs=placed, out_specs=P("row", "col", None), check_vma=False
    )
```

profile of v0, /device:TPU:1, one launch (start us, length us, event | category | flops | bytes accessed | tf_op | source)
XLA Modules:
  0.0 358.9 jit_solution(2798819045864562003)
XLA Ops:
  6.5 0.0 copy-start
  6.5 20.3 %all-gather = s32[16,24,2]{1,2,0:T(2,128)S(1)} all-gather(s32[1,24,2]{1,2,0:T(2,128)} %bitcast.26), channel_id=1, replica_groups=mesh['row'=16,'col'=8] {'row'}, dimensions={0}, use_global_device_ids=true | all-gather | bytes 3264 | tf_op jit(solution)/shard_map/all_gather | solution.py:15
  26.8 0.1 reshape.79
  27.0 0.1 reduce_max.15
  27.0 0.1 reduce_max.20
  27.2 6.2 %gather_fusion = bf16[16,256,1024]{2,1,0:T(8,128)(2,1)} fusion(bf16[4,256,1024]{2,1,0:T(8,128)(2,1)} %bitcast.24, s32[1024]{0:T(1024)S(1)} %pad_clamp_fusion.1), kind=kCustom, calls=%fused_computation.2 | custom fusion | bytes 16777280 | tf_op jit(solution)/shard_map/jit(_take)/gather | solution.py:20
  33.4 7.4 %broadcast_select_fusion.1 = bf16[16,256,1024]{2,1,0:T(8,128)(2,1)} fusion(bf16[16,256,1024]{2,1,0:T(8,128)(2,1)} %gather_fusion, pred[16]{0:T(512)(128)(4,1)S(1)} %compare_and_fusion.1), kind=kLoop, calls=%fused_computation.13 | loop fusion | flops 4194304 | bytes 16777232 | tf_op jit(solution)/shard_map/jit(_take)/select_n | solution.py:20
  40.9 0.0 copy-start.3
  40.9 4.9 %all-to-all-start = ((bf16[16,256,1024]{2,1,0:T(8,128)(2,1)}), bf16[16,256,1024]{2,1,0:T(8,128)(2,1)}, u32[]{:S(2)}, u32[]{:S(2)}) async-start(bf16[16,256,1024]{2,1,0:T(8,128)(2,1)} %broadcast_select_fusion.1), calls=%async_computation | async-start | bytes 16777216 | tf_op jit(solution)/shard_map/all_to_all | solution.py:21
  45.8 0.0 all-reduce.2.cloned.1.call-start
  45.9 0.0 copy-done.3
  45.9 0.0 copy-done
  45.9 6.0 %gather_fusion.2 = bf16[24,256,1024]{2,1,0:T(8,128)(2,1)} fusion(bf16[4,256,1024]{2,1,0:T(8,128)(2,1)S(1)} %bitcast.22, s32[1024]{0:T(1024)S(1)} %pad_clamp_fusion.2), kind=kCustom, calls=%fused_computation.clone | custom fusion | bytes 25165920 | tf_op jit(solution)/shard_map/jit(_take)/gather | solution.py:29
  51.9 0.0 copy-start.2
  51.9 7.8 %gather_fusion.3 = bf16[24,256,1024]{2,1,0:T(8,128)(2,1)} fusion(bf16[4,256,1024]{2,1,0:T(8,128)(2,1)} %bitcast.23, s32[1024]{0:T(1024)S(1)} %pad_clamp_fusion.2), kind=kCustom, calls=%fused_computation.1.clone | custom fusion | bytes 25165920 | tf_op jit(solution)/shard_map/jit(_take)/gather | solution.py:30
  59.7 83.6 %all-to-all-done = bf16[16,256,1024]{2,1,0:T(8,128)(2,1)} async-done(((bf16[16,256,1024]{2,1,0:T(8,128)(2,1)}), bf16[16,256,1024]{2,1,0:T(8,128)(2,1)}, u32[]{:S(2)}, u32[]{:S(2)}) %all-to-all-start) | async-done | bytes 8388640 | tf_op jit(solution)/shard_map/all_to_all | solution.py:21
  143.4 0.0 copy-done.2
  143.4 8.6 %pad_maximum_fusion.1 = bf16[20,256,1024]{2,1,0:T(8,128)(2,1)} fusion(bf16[16,256,1024]{2,1,0:T(8,128)(2,1)} %all-to-all-done, bf16[4,256,1024]{2,1,0:T(8,128)(2,1)S(1)} %bitcast.25), kind=kLoop, calls=%fused_computation.12 | loop fusion | flops 5242880 | bytes 20971520 | tf_op jit(solution)/shard_map/concatenate | solution.py:22
  152.0 10.1 %gather_fusion.1 = bf16[24,256,1024]{2,1,0:T(8,128)(2,1)} fusion(bf16[20,256,1024]{2,1,0:T(8,128)(2,1)} %pad_maximum_fusion.1, s32[1024]{0:T(1024)S(1)} %pad_clamp_fusion), kind=kCustom, calls=%fused_computation.3 | custom fusion | bytes 25165920 | tf_op jit(solution)/shard_map/jit(_take)/gather | solution.py:31
  162.1 13.1 %fusion.8 = f32[1,24,256,256]{3,2,1,0:T(8,128)} fusion(bf16[24,256,1024]{2,1,0:T(8,128)(2,1)} %gather_fusion.1, pred[24]{0:T(512)(128)(4,1)S(1)} %get-tuple-element.8, bf16[24,256,1024]{2,1,0:T(8,128)(2,1)} %gather_fusion.2, pred[24]{0:T(512)(128)(4,1)S(1)} %get-tuple-element.6), kind=kOutput, calls=%fused_computation.16 | convolution fusion | flops 3233808384 | bytes 31457328 | tf_op jit(solution)/shard_map/tak,tbk->tab/dot_general | solution.py:32
  175.1 13.0 %fusion.11 = f32[1,24,256,256]{3,2,1,0:T(8,128)} fusion(bf16[24,256,1024]{2,1,0:T(8,128)(2,1)} %gather_fusion.1, pred[24]{0:T(512)(128)(4,1)S(1)} %get-tuple-element.8, bf16[24,256,1024]{2,1,0:T(8,128)(2,1)} %gather_fusion.3, pred[24]{0:T(512)(128)(4,1)S(1)} %get-tuple-element.6), kind=kOutput, calls=%fused_computation.17 | convolution fusion | flops 3233808384 | bytes 31457328 | tf_op jit(solution)/shard_map/tak,tbk->tab/dot_general | solution.py:33
  188.2 0.0 copy-start.1
  188.2 10.7 %pad_maximum_fusion = f32[2,24,256,256]{3,2,1,0:T(8,128)} fusion(f32[1,24,256,256]{3,2,1,0:T(8,128)} %fusion.11, f32[1,24,256,256]{3,2,1,0:T(8,128)} %fusion.8), kind=kLoop, calls=%fused_computation.4 | loop fusion | flops 3145728 | bytes 25165824 | tf_op jit(solution)/shard_map/stack | solution.py:34
  198.9 0.0 all-reduce.2.cloned.1.call-update
  198.9 150.7 %all-reduce.2.cloned.1.call-done = f32[2,24,256,256]{3,2,1,0:T(8,128)} async-done(((f32[2,24,256,256]{3,2,1,0:T(8,128)}), f32[2,24,256,256]{3,2,1,0:T(8,128)}) %all-reduce.2.cloned.1.call-update) | async-done | bytes 12582928 | tf_op jit(solution)/shard_map/psum | solution.py:35
  349.6 2.4 fusion.14
  352.0 0.0 copy-done.1
  (9 shorter events, 0.1 us)
Async XLA Ops:
  6.5 39.4 %copy-start = (bf16[1024,1024]{1,0:T(8,128)(2,1)S(1)}, bf16[1024,1024]{1,0:T(8,128)(2,1)}, u32[]{:S(2)}) copy-start(bf16[1024,1024]{1,0:T(8,128)(2,1)} %param.6) | copy-start | bytes 6291460
  40.9 5.0 %copy-start.3 = (s32[24,2]{0,1:T(2,128)S(1)}, s32[24,2]{0,1:T(2,128)}, u32[]{:S(2)}) copy-start(s32[24,2]{0,1:T(2,128)} %param.9) | copy-start | bytes 580
  40.9 102.5 %all-to-all-start = ((bf16[16,256,1024]{2,1,0:T(8,128)(2,1)}), bf16[16,256,1024]{2,1,0:T(8,128)(2,1)}, u32[]{:S(2)}, u32[]{:S(2)}) async-start(bf16[16,256,1024]{2,1,0:T(8,128)(2,1)} %broadcast_select_fusion.1), calls=%async_computation | async-start | bytes 16777216 | tf_op jit(solution)/shard_map/all_to_all | solution.py:21
  45.8 303.8 %all-reduce.2.cloned.1.call-start = ((), (), s32[]{:S(2)}) async-start(), calls=%async_computation.1 | async-start | bytes 25165824 | tf_op jit(solution)/shard_map/psum | solution.py:35
  51.9 91.5 %copy-start.2 = (bf16[1024,1024]{1,0:T(8,128)(2,1)S(1)}, bf16[1024,1024]{1,0:T(8,128)(2,1)}, u32[]{:S(2)}) copy-start(bf16[1024,1024]{1,0:T(8,128)(2,1)} %param.8) | copy-start | bytes 6291460
  188.2 163.8 %copy-start.1 = (bf16[1024,1024]{1,0:T(8,128)(2,1)S(1)}, bf16[1024,1024]{1,0:T(8,128)(2,1)}, u32[]{:S(2)}) copy-start(bf16[1024,1024]{1,0:T(8,128)(2,1)} %param.6) | copy-start | bytes 6291460
Sparse Core Ops, SparseCore 0:
  199.1 150.5 all-reduce.1
where the time goes:
time: 359 us
  waiting for transfers between devices  234 us (65%)
  local copies, waits for them, and re-layouts  30.3 us (8%)
  other arithmetic  29.4 us (8%)
  matrix products  26.1 us (7%)
  blocking collectives  20.3 us (6%)
  between operations  13.5 us (4%)
  starting transfers between devices  4.98 us (1%)
    psum x1, waiting for transfers between devices, shards(): whole = lax.psum(stacked, 'col')  151 us
    all_to_all x1, waiting for transfers between devices, shards(): lax.all_to_all(outgoing, 'row', split_axis=0, concat_axis=0, tiled=True)  83.6 us
    all_gather x1, blocking collectives, shards(): every_pair = lax.all_gather(pairs, 'row', axis=0, tiled=True)  20.3 us
    dot_general x1, matrix products, shards(): jnp.einsum('tak,tbk->tab', left_x, right_rows, preferred_element_type=jnp...  13.1 us
    dot_general x1, matrix products, shards(): jnp.einsum('tak,tbk->tab', left_s, right_rows, preferred_element_type=jnp...  13 us
    another operation x1, other arithmetic, shards(): stacked = jnp.stack([cross_x, cross_s])  10.7 us
    gather x1, local copies, waits for them, and re-layouts, shards(): right_rows = jnp.take(block_table, second_slot, axis=0)  10.1 us
    concatenate x1, other arithmetic, shards(): block_table = jnp.concatenate([weight_blocks, incoming], axis=0)  8.62 us
  transfers between devices with their start and end apart: 2, of which 2 were waited for; matrix products, arithmetic and copies ran while one was open for 4% of the time, Pallas kernels for 0%

commit v1 on v0

--- a/solution.py
+++ b/solution.py
@@ -32,7 +32,12 @@
     cross_x = jnp.einsum("tak,tbk->tab", left_x, right_rows, preferred_element_type=jnp.float32)
     cross_s = jnp.einsum("tak,tbk->tab", left_s, right_rows, preferred_element_type=jnp.float32)
     stacked = jnp.stack([cross_x, cross_s])
-    whole = lax.psum(stacked, "col")
+
+    def edit_numbers(block_here, shard_axis):
+        side_arr = jnp.sum(jax.lax.all_gather(block_here, shard_axis), axis=0)
+        return side_arr
+
+    whole = edit_numbers(stacked, "col")
     slice_rows = TILE // lax.axis_size("col")
     summed = lax.dynamic_slice_in_dim(whole, lax.axis_index("col") * slice_rows, slice_rows, 2)
     return summed[0] * summed[1]

time: 359 us -> 690 us (1.92)
  waiting for transfers between devices: 234 us -> 529 us
  other arithmetic: 29.4 us -> 65.1 us
    all_gather x0 -> x1, waiting for transfers between devices: none -> 446 us  [edit_numbers(): side_arr = jnp.sum(jax.lax.all_gather(block_here, shard_axis), axis=0)]
    psum x1 -> x0, waiting for transfers between devices: 151 us -> none  [shards(): whole = lax.psum(stacked, 'col')]
    reduce_sum x0 -> x1, other arithmetic: none -> 35.9 us  [edit_numbers(): side_arr = jnp.sum(jax.lax.all_gather(block_here, shard_axis), axis=0)]
  transfers between devices with their start and end apart: 2 -> 2, of which waited for: 2 -> 2; matrix products, arithmetic and copies ran while one was open for 4% -> 2% of each run, Pallas kernels for 0% -> 0%
where the time goes in v1:
time: 690 us
  waiting for transfers between devices  529 us (77%)
  other arithmetic  65.1 us (9%)
  local copies, waits for them, and re-layouts  30.3 us (4%)
  matrix products  26.1 us (4%)
  blocking collectives  20.3 us (3%)
  between operations  13.5 us (2%)
    all_gather x1, waiting for transfers between devices, edit_numbers(): side_arr = jnp.sum(jax.lax.all_gather(block_here, shard_axis), axis=0)  446 us
    all_to_all x1, waiting for transfers between devices, shards(): lax.all_to_all(outgoing, 'row', split_axis=0, concat_axis=0, tiled=True)  83.6 us
    reduce_sum x1, other arithmetic, edit_numbers(): side_arr = jnp.sum(jax.lax.all_gather(block_here, shard_axis), axis=0)  35.9 us
    all_gather x1, blocking collectives, shards(): every_pair = lax.all_gather(pairs, 'row', axis=0, tiled=True)  20.3 us
  transfers between devices with their start and end apart: 2, of which 2 were waited for; matrix products, arithmetic and copies ran while one was open for 2% of the time, Pallas kernels for 0%

profile of v1, /device:TPU:1, one launch (start us, length us, event | category | flops | bytes accessed | tf_op | source)
XLA Modules:
  0.0 689.6 jit_solution(8684105692919679544)
XLA Ops:
  6.5 0.0 copy-start
  6.5 20.3 %all-gather.1 = s32[16,24,2]{1,2,0:T(2,128)S(1)} all-gather(s32[1,24,2]{1,2,0:T(2,128)} %bitcast.27), channel_id=1, replica_groups=mesh['row'=16,'col'=8] {'row'}, dimensions={0}, use_global_device_ids=true | all-gather | bytes 3264 | tf_op jit(solution)/shard_map/all_gather | solution.py:15
  26.8 0.1 reshape.80
  27.0 0.1 reduce_max.15
  27.0 0.1 reduce_max.20
  27.2 6.2 gather_fusion
  33.4 7.4 %broadcast_select_fusion.1 = bf16[16,256,1024]{2,1,0:T(8,128)(2,1)} fusion(bf16[16,256,1024]{2,1,0:T(8,128)(2,1)} %gather_fusion, pred[16]{0:T(512)(128)(4,1)S(1)} %compare_and_fusion.1), kind=kLoop, calls=%fused_computation.13 | loop fusion | flops 4194304 | bytes 16777232 | tf_op jit(solution)/shard_map/jit(_take)/select_n | solution.py:20
  40.9 0.0 copy-start.3
  40.9 4.9 all-to-all-start
  45.8 0.0 all-gather.4.cloned.1.call-start
  45.9 0.0 copy-done.3
  45.9 0.0 copy-done
  45.9 6.0 gather_fusion.2
  51.9 0.0 copy-start.2
  51.9 7.8 %gather_fusion.3 = bf16[24,256,1024]{2,1,0:T(8,128)(2,1)} fusion(bf16[4,256,1024]{2,1,0:T(8,128)(2,1)} %bitcast.24, s32[1024]{0:T(1024)S(1)} %pad_clamp_fusion.2), kind=kCustom, calls=%fused_computation.1.clone | custom fusion | bytes 25165920 | tf_op jit(solution)/shard_map/jit(_take)/gather | solution.py:30
  59.7 83.6 %all-to-all-done = bf16[16,256,1024]{2,1,0:T(8,128)(2,1)} async-done(((bf16[16,256,1024]{2,1,0:T(8,128)(2,1)}), bf16[16,256,1024]{2,1,0:T(8,128)(2,1)}, u32[]{:S(2)}, u32[]{:S(2)}) %all-to-all-start) | async-done | bytes 8388640 | tf_op jit(solution)/shard_map/all_to_all | solution.py:21
  143.4 0.0 copy-done.2
  143.4 8.6 %pad_maximum_fusion.1 = bf16[20,256,1024]{2,1,0:T(8,128)(2,1)} fusion(bf16[16,256,1024]{2,1,0:T(8,128)(2,1)} %all-to-all-done, bf16[4,256,1024]{2,1,0:T(8,128)(2,1)S(1)} %bitcast.26), kind=kLoop, calls=%fused_computation.12 | loop fusion | flops 5242880 | bytes 20971520 | tf_op jit(solution)/shard_map/concatenate | solution.py:22
  152.0 10.1 %gather_fusion.1 = bf16[24,256,1024]{2,1,0:T(8,128)(2,1)} fusion(bf16[20,256,1024]{2,1,0:T(8,128)(2,1)} %pad_maximum_fusion.1, s32[1024]{0:T(1024)S(1)} %pad_clamp_fusion), kind=kCustom, calls=%fused_computation.3 | custom fusion | bytes 25165920 | tf_op jit(solution)/shard_map/jit(_take)/gather | solution.py:31
  162.1 13.1 %fusion.8 = f32[1,24,256,256]{3,2,1,0:T(8,128)} fusion(bf16[24,256,1024]{2,1,0:T(8,128)(2,1)} %gather_fusion.1, pred[24]{0:T(512)(128)(4,1)S(1)} %get-tuple-element.8, bf16[24,256,1024]{2,1,0:T(8,128)(2,1)} %gather_fusion.2, pred[24]{0:T(512)(128)(4,1)S(1)} %get-tuple-element.6), kind=kOutput, calls=%fused_computation.16 | convolution fusion | flops 3233808384 | bytes 31457328 | tf_op jit(solution)/shard_map/tak,tbk->tab/dot_general | solution.py:32
  175.1 13.0 %fusion.11 = f32[1,24,256,256]{3,2,1,0:T(8,128)} fusion(bf16[24,256,1024]{2,1,0:T(8,128)(2,1)} %gather_fusion.1, pred[24]{0:T(512)(128)(4,1)S(1)} %get-tuple-element.8, bf16[24,256,1024]{2,1,0:T(8,128)(2,1)} %gather_fusion.3, pred[24]{0:T(512)(128)(4,1)S(1)} %get-tuple-element.6), kind=kOutput, calls=%fused_computation.17 | convolution fusion | flops 3233808384 | bytes 31457328 | tf_op jit(solution)/shard_map/tak,tbk->tab/dot_general | solution.py:33
  188.2 10.5 %pad_maximum_fusion = f32[2,24,256,256]{3,2,1,0:T(8,128)} fusion(f32[1,24,256,256]{3,2,1,0:T(8,128)} %fusion.11, f32[1,24,256,256]{3,2,1,0:T(8,128)} %fusion.8), kind=kLoop, calls=%fused_computation.4 | loop fusion | flops 3145728 | bytes 25165824 | tf_op jit(solution)/shard_map/stack | solution.py:34
  198.7 0.0 all-gather.4.cloned.1.call-update
  198.7 445.7 %all-gather.4.cloned.1.call-done = f32[16,24,256,256]{3,2,1,0:T(8,128)} async-done(((f32[2,24,256,256]{3,2,1,0:T(8,128)}), f32[16,24,256,256]{3,2,1,0:T(8,128)}) %all-gather.4.cloned.1.call-update) | async-done | bytes 100663312 | tf_op jit(solution)/shard_map/all_gather | solution.py:37
  644.4 0.0 copy-start.1
  644.4 35.9 %reduce_sum.9 = f32[2,24,256,256]{3,2,1,0:T(8,128)} reduce(f32[8,2,24,256,256]{4,3,2,1,0:T(8,128)} %bitcast.11, f32[]{:T(128)} %constant.78.clone.1), dimensions={0}, to_apply=%region_2.4 | reduce | flops 22020096 | bytes 113246208 | tf_op jit(solution)/shard_map/reduce_sum | solution.py:37
  680.3 2.4 fusion.14
  682.7 0.0 copy-done.1
  (9 shorter events, 0.1 us)
Async XLA Ops:
  6.5 39.4 %copy-start = (bf16[1024,1024]{1,0:T(8,128)(2,1)S(1)}, bf16[1024,1024]{1,0:T(8,128)(2,1)}, u32[]{:S(2)}) copy-start(bf16[1024,1024]{1,0:T(8,128)(2,1)} %param.6) | copy-start | bytes 6291460
  40.9 5.0 copy-start.3
  40.9 102.5 %all-to-all-start = ((bf16[16,256,1024]{2,1,0:T(8,128)(2,1)}), bf16[16,256,1024]{2,1,0:T(8,128)(2,1)}, u32[]{:S(2)}, u32[]{:S(2)}) async-start(bf16[16,256,1024]{2,1,0:T(8,128)(2,1)} %broadcast_select_fusion.1), calls=%async_computation | async-start | bytes 16777216 | tf_op jit(solution)/shard_map/all_to_all | solution.py:21
  45.8 598.6 %all-gather.4.cloned.1.call-start = ((), (), s32[]{:S(2)}) async-start(), calls=%async_computation.1 | async-start | bytes 113246208 | tf_op jit(solution)/shard_map/all_gather | solution.py:37
  51.9 91.5 %copy-start.2 = (bf16[1024,1024]{1,0:T(8,128)(2,1)S(1)}, bf16[1024,1024]{1,0:T(8,128)(2,1)}, u32[]{:S(2)}) copy-start(bf16[1024,1024]{1,0:T(8,128)(2,1)} %param.8) | copy-start | bytes 6291460
  644.4 38.3 %copy-start.1 = (bf16[1024,1024]{1,0:T(8,128)(2,1)S(1)}, bf16[1024,1024]{1,0:T(8,128)(2,1)}, u32[]{:S(2)}) copy-start(bf16[1024,1024]{1,0:T(8,128)(2,1)} %param.6) | copy-start | bytes 6291460
Sparse Core Ops, SparseCore 0:
  198.9 445.5 all-gather.3
